TPU v7x, 512 devices: a whole 4x8x8 slice. The times are simulated.
512 devices in a mesh: tm: 64 (over y, x, z_lo), run: 8 (over z_hi, core).
Axes of the slice: x: 4, y: 8, z: 8 (z_hi: 4, z_lo: 2; z = z_hi * 2 + z_lo), core: 2. Of those that a mesh axis runs over, the one named last changes fastest.
Arguments:
- signal: bfloat16 [8, 65536, 256], P('run', 'tm'), may hold values from -6 to 6
- conv_weight: bfloat16 [768, 512], replicated, may hold values from -0.21875 to 0.21875
- conv_bias: float32 [512], replicated, may hold values from -3 to 3
- out_weight: bfloat16 [256, 256], replicated, may hold values from -0.375 to 0.375
- out_bias: float32 [256], replicated, may hold values from -3 to 3
- cotangent: bfloat16 [8, 65536, 256], P('run', 'tm'), may hold values from -8 to 8
Outputs:
- output: bfloat16 [8, 65536, 256], P('run', 'tm')
- grad_signal: bfloat16 [8, 65536, 256], P('run', 'tm')
- grad_conv_weight: float32 [768, 512], replicated
- grad_conv_bias: float32 [512], replicated
- grad_out_weight: float32 [256, 256], replicated
- grad_out_bias: float32 [256], replicated
All inputs are finite; a program needn't handle non-finite values.
Results may differ from a plain program's by a relative error of at most 0.0034.
Values may be sent and summed in bfloat16 or wider, within the bound.
A program may use at most 64 MiB of HBM per device.

v0:
```python
import jax
import jax.numpy as jnp
from jax import lax
from jax.sharding import PartitionSpec as P

DILATION_STEPS = 256
KERNEL_TAPS = 3


def passed_along(array, axis, by):
    size = lax.axis_size(axis)
    pairs = [(i, i + by) for i in range(size) if 0 <= i + by < size]
    return lax.ppermute(array, axis, pairs)


def local(signal, conv_weight, conv_bias, out_weight, out_bias, cotangent):
    device_rows = signal.shape[1]
    channels = signal.shape[2]
    receptive_span = (KERNEL_TAPS - 1) * DILATION_STEPS
    history = passed_along(signal[:, device_rows - receptive_span :, :], "tm", 1)
    padded_input = jnp.concatenate([history, signal], 1)
    tap_stack = jnp.concatenate(
        [
            padded_input[
                :,
                receptive_span
                - kernel_tap_index * DILATION_STEPS : receptive_span
                - kernel_tap_index * DILATION_STEPS
                + device_rows,
            ]
            for kernel_tap_index in range(KERNEL_TAPS)
        ],
        2,
    )
    preact = (
        jnp.einsum("bsk,kn->bsn", tap_stack, conv_weight, preferred_element_type=jnp.float32)
        + conv_bias
    )
    filtered = jnp.tanh(preact[..., :channels])
    gated = jax.nn.sigmoid(preact[..., channels:])
    mixed = (filtered * gated).astype(jnp.bfloat16)
    hidden = (
        jnp.einsum("bsc,cd->bsd", mixed, out_weight, preferred_element_type=jnp.float32) + out_bias
    )
    output = (signal.astype(jnp.float32) + hidden).astype(jnp.bfloat16)
    dmixed = jnp.einsum("bsd,cd->bsc", cotangent, out_weight, preferred_element_type=jnp.float32)
    dpre = jnp.concatenate(
        [dmixed * gated * (1.0 - filtered * filtered), dmixed * filtered * gated * (1.0 - gated)], 2
    ).astype(jnp.bfloat16)
    dstacked = jnp.einsum("bsn,kn->bsk", dpre, conv_weight, preferred_element_type=jnp.float32)
    local_grad = jnp.zeros((signal.shape[0], receptive_span + device_rows, channels), jnp.float32)
    for kernel_tap_index in range(KERNEL_TAPS):
        shifted_slice = dstacked[
            ..., kernel_tap_index * channels : (kernel_tap_index + 1) * channels
        ]
        local_grad = local_grad + jnp.pad(
            shifted_slice,
            (
                (0, 0),
                (
                    receptive_span - kernel_tap_index * DILATION_STEPS,
                    kernel_tap_index * DILATION_STEPS,
                ),
                (0, 0),
            ),
        )
    incoming = passed_along(local_grad[:, :receptive_span].astype(jnp.bfloat16), "tm", -1).astype(
        jnp.float32
    )
    grad_signal = (
        cotangent.astype(jnp.float32)
        + local_grad[:, receptive_span:]
        + jnp.pad(incoming, ((0, 0), (device_rows - receptive_span, 0), (0, 0)))
    )
    grad_signal = grad_signal.astype(jnp.bfloat16)
    grad_conv = jnp.einsum("bsk,bsn->kn", tap_stack, dpre, preferred_element_type=jnp.float32)
    grad_cbias = jnp.sum(dpre.astype(jnp.float32), (0, 1))
    grad_proj = jnp.einsum("bsc,bsd->cd", mixed, cotangent, preferred_element_type=jnp.float32)
    grad_pbias = jnp.sum(cotangent.astype(jnp.float32), (0, 1))
    scale = float(signal.shape[0] * lax.axis_size("run") * device_rows * lax.axis_size("tm")) ** (
        -0.5
    )
    summed = lax.psum((grad_conv, grad_cbias, grad_proj, grad_pbias), ("tm", "run"))
    return (
        output,
        grad_signal,
        summed[0] * scale,
        summed[1] * scale,
        summed[2] * scale,
        summed[3] * scale,
    )


def solution(mesh):
    placed = (P("run", "tm", None), P(), P(), P(), P(), P("run", "tm", None))
    return jax.shard_map(
        local,
        mesh=mesh,
        in_specs=placed,
        out_specs=(P("run", "tm", None), P("run", "tm", None), P(), P(), P(), P()),
        check_vma=False,
    )
```

profile of v0, /device:TPU:1, one launch (start us, length us, event | category | flops | bytes accessed | tf_op | source)
XLA Modules:
  0.0 329.9 jit_solution(11281328637928422365)
XLA Ops:
  7.2 0.0 copy-start
  7.2 0.0 copy-start.2
  7.2 0.0 copy-start.6
  7.2 0.0 all-reduce.8.cloned.1.call-start
  7.2 1.1 slice.31
  8.3 4.8 %collective-permute-start = (bf16[1,512,256]{2,1,0:T(8,128)(2,1)S(1)}, bf16[1,512,256]{2,1,0:T(8,128)(2,1)S(1)}, u32[]{:S(2)}, u32[]{:S(2)}) collective-permute-start(bf16[1,512,256]{2,1,0:T(8,128)(2,1)S(1)} %slice.31), channel_id=1, source_target_pairs={{0,8},{8,16},{16,24},{24,32},{32,40},{40,48},{48,56},{56,64},{64,7... | collective-permute-start | bytes 786440 | tf_op jit(solution)/shard_map/ppermute | solution.py:13
  13.2 3.3 collective-permute-done
  16.5 1.1 constant_dynamic-update-slice_fusion
  17.5 0.1 fusion.17
  17.6 0.0 copy-done
  17.6 0.0 copy-done.2
  17.6 0.0 copy-done.6
  17.7 0.0 copy-start.1
  17.7 0.0 copy-start.5
  17.7 1.0 add_bitcast_fusion
  18.7 0.0 copy-done.1
  18.7 0.0 copy-done.5
  18.7 0.8 multiply_convert_fusion.1
  19.5 0.0 copy-start.3
  19.5 0.2 convert_reduce_fusion
  19.8 2.2 fusion.8
  21.9 2.7 convolution_bitcast_fusion
  24.6 0.0 copy-done.3
  24.6 1.0 fusion.10
  25.6 2.1 fusion.16
  27.7 0.2 pad_add_fusion
  27.9 0.0 copy-start.7
  27.9 0.7 slice.74
  28.7 1.3 collective-permute-start.1
  30.0 0.0 all-reduce.8.cloned.1.call-update
  30.0 0.0 copy-done.7
  30.0 2.2 fusion.2
  32.2 4.4 %collective-permute-done.1 = bf16[1,512,256]{2,1,0:T(8,128)(2,1)} collective-permute-done((bf16[1,512,256]{2,1,0:T(8,128)(2,1)}, bf16[1,512,256]{2,1,0:T(8,128)(2,1)}, u32[]{:S(2)}, u32[]{:S(2)}) %collective-permute-start.1) | collective-permute-done | bytes 262176 | tf_op jit(solution)/shard_map/ppermute | solution.py:13
  36.6 2.0 convert_reduce_fusion.1
  38.6 113.1 %all-reduce.4 = (f32[512]{0:T(512)S(1)}, f32[256]{0:T(256)S(1)}) all-reduce(f32[512]{0:T(512)S(1)} %convert_reduce_fusion, f32[256]{0:T(256)S(1)} %get-tuple-element.18), channel_id=1, replica_groups=mesh['tm'=64,'run'=8] {'tm','run'}, use_global_device_ids=true, to_apply=%region_2.3 | all-reduce | flops 768 | bytes 6144 | tf_op jit(solution)/shard_map/psum | solution.py:83
  151.6 0.6 broadcast_multiply_fusion.3
  152.2 0.6 broadcast_multiply_fusion.2
  152.8 166.8 %all-reduce.8.cloned.1.call-done = (f32[768,512]{1,0:T(8,128)}, f32[256,256]{1,0:T(8,128)}) async-done(((f32[768,512]{1,0:T(8,128)}, f32[256,256]{1,0:T(8,128)}), (f32[768,512]{1,0:T(8,128)}, f32[256,256]{1,0:T(8,128)})) %all-reduce.8.cloned.1.call-update) | async-done | bytes 1835024 | tf_op jit(solution)/shard_map/psum | solution.py:83
  319.5 0.0 copy-start.4
  319.5 2.8 broadcast_multiply_fusion
  322.3 0.0 copy-done.4
  322.3 0.7 broadcast_multiply_fusion.1
  (1 shorter events, 0.0 us)
Async XLA Ops:
  7.2 10.5 %copy-start = (bf16[768,512]{1,0:T(8,128)(2,1)S(1)}, bf16[768,512]{1,0:T(8,128)(2,1)}, u32[]{:S(2)}) copy-start(bf16[768,512]{1,0:T(8,128)(2,1)} %param.7) | copy-start | bytes 2359300
  7.2 10.5 %copy-start.2 = (bf16[1,1024,256]{2,1,0:T(8,128)(2,1)S(1)}, bf16[1,1024,256]{2,1,0:T(8,128)(2,1)}, u32[]{:S(2)}) copy-start(bf16[1,1024,256]{2,1,0:T(8,128)(2,1)} %param.6) | copy-start | bytes 1572868
  7.2 10.5 %copy-start.6 = (f32[512]{0:T(512)S(1)}, f32[512]{0:T(512)}, u32[]{:S(2)}) copy-start(f32[512]{0:T(512)} %param.8) | copy-start | bytes 6148
  7.2 312.3 %all-reduce.8.cloned.1.call-start = ((), (), s32[]{:S(2)}) async-start(), calls=%async_computation | async-start | bytes 3670016 | tf_op jit(solution)/shard_map/psum | solution.py:83
  8.3 8.1 %collective-permute-start = (bf16[1,512,256]{2,1,0:T(8,128)(2,1)S(1)}, bf16[1,512,256]{2,1,0:T(8,128)(2,1)S(1)}, u32[]{:S(2)}, u32[]{:S(2)}) collective-permute-start(bf16[1,512,256]{2,1,0:T(8,128)(2,1)S(1)} %slice.31), channel_id=1, source_target_pairs={{0,8},{8,16},{16,24},{24,32},{32,40},{40,48},{48,56},{56,64},{64,7... | collective-permute-start | bytes 786440 | tf_op jit(solution)/shard_map/ppermute | solution.py:13
  17.7 1.1 copy-start.1
  17.7 1.1 copy-start.5
  19.5 5.1 %copy-start.3 = (bf16[1024,256]{0,1:T(8,128)(2,1)}, bf16[1024,256]{0,1:T(8,128)(2,1)S(1)}, u32[]{:S(2)}) copy-start(bf16[1024,256]{0,1:T(8,128)(2,1)S(1)} %get-tuple-element.15) | copy-start | bytes 1572868
  27.9 2.1 copy-start.7
  28.7 7.9 %collective-permute-start.1 = (bf16[1,512,256]{2,1,0:T(8,128)(2,1)}, bf16[1,512,256]{2,1,0:T(8,128)(2,1)}, u32[]{:S(2)}, u32[]{:S(2)}) collective-permute-start(bf16[1,512,256]{2,1,0:T(8,128)(2,1)} %slice.74), channel_id=1, source_target_pairs={{8,0},{16,8},{24,16},{32,24},{40,32},{48,40},{56,48},{64,56},{72,6... | collective-permute-start | bytes 786440 | tf_op jit(solution)/shard_map/ppermute | solution.py:13
  319.5 2.8 copy-start.4
Sparse Core Ops, SparseCore 0:
  30.1 289.3 all-reduce.7
where the time goes:
time: 330 us
  waiting for transfers between devices  174 us (53%)
  blocking collectives  113 us (34%)
  between operations  14.2 us (4%)
  matrix products  9.89 us (3%)
  other arithmetic  7.02 us (2%)
  starting transfers between devices  6.16 us (2%)
  local copies, waits for them, and re-layouts  5.08 us (2%)
    psum x1, waiting for transfers between devices, local(): lax.psum((grad_conv, grad_cbias, grad_proj, grad_pbias), ('tm', 'run'))  167 us
    psum x1, blocking collectives, local(): lax.psum((grad_conv, grad_cbias, grad_proj, grad_pbias), ('tm', 'run'))  113 us
    ppermute x2, waiting for transfers between devices, passed_along(): return lax.ppermute(array, axis, pairs)  7.68 us
  transfers between devices with their start and end apart: 3, of which 3 were waited for; matrix products, arithmetic and copies ran while one was open for 2% of the time, Pallas kernels for 0%

commit v1 on v0

--- a/solution.py
+++ b/solution.py
@@ -80,7 +80,7 @@
     scale = float(signal.shape[0] * lax.axis_size("run") * device_rows * lax.axis_size("tm")) ** (
         -0.5
     )
-    summed = lax.psum((grad_conv, grad_cbias, grad_proj, grad_pbias), ("tm", "run"))
+    summed = lax.psum(lax.psum((grad_conv, grad_cbias, grad_proj, grad_pbias), "tm"), "run")
     return (
         output,
         grad_signal,

time: 330 us -> 832 us (2.52)
  waiting for transfers between devices: 174 us -> 580 us
  blocking collectives: 113 us -> 211 us
    psum x1 -> x2, waiting for transfers between devices: 167 us -> 572 us  [the longest x1 572 us: local(): lax.psum((grad_conv, grad_cbias, grad_proj, grad_pbias), 'tm')]
    psum x1 -> x2, blocking collectives: 113 us -> 211 us  [the longest x1 126 us: local(): lax.psum((grad_conv, grad_cbias, grad_proj, grad_pbias), 'tm')]
  transfers between devices with their start and end apart: 3 -> 4, of which waited for: 3 -> 3; matrix products, arithmetic and copies ran while one was open for 2% -> 1% of each run, Pallas kernels for 0% -> 0%
where the time goes in v1:
time: 832 us; the launch traced here: 828 us
  waiting for transfers between devices  580 us (70%)
  blocking collectives  211 us (25%)
  between operations  14.2 us (2%)
    psum x1, waiting for transfers between devices, local(): lax.psum((grad_conv, grad_cbias, grad_proj, grad_pbias), 'tm')  572 us
    psum x1, blocking collectives, local(): lax.psum((grad_conv, grad_cbias, grad_proj, grad_pbias), 'tm')  126 us
    psum x1, blocking collectives, local(): lax.psum(lax.psum((grad_conv, grad_cbias, grad_proj, grad_pbias), 'tm'),...  84.9 us
  transfers between devices with their start and end apart: 4, of which 3 were waited for; matrix products, arithmetic and copies ran while one was open for 1% of the time, Pallas kernels for 0%

profile of v1, /device:TPU:1, one launch (start us, length us, event | category | flops | bytes accessed | tf_op | source)
XLA Modules:
  0.0 827.5 jit_solution(1950317493220529019)
XLA Ops:
  7.2 0.0 copy-start
  7.2 0.0 copy-start.2
  7.2 0.0 copy-start.5
  7.2 0.0 all-reduce.11.cloned.1.call-start
  7.3 1.1 slice.31
  8.3 4.8 collective-permute-start
  13.2 3.3 collective-permute-done
  16.5 1.1 constant_dynamic-update-slice_fusion
  17.5 0.1 fusion.17
  17.6 0.0 copy-done
  17.6 0.0 copy-done.2
  17.6 0.0 copy-done.5
  17.7 0.0 copy-start.1
  17.7 0.0 copy-start.4
  17.7 1.0 add_bitcast_fusion
  18.7 0.0 copy-done.1
  18.7 0.0 copy-done.4
  18.7 0.8 multiply_convert_fusion.1
  19.5 1.0 fusion.10
  20.5 2.2 fusion.8
  22.7 0.0 all-reduce.11.cloned.1.call-update
  22.7 0.0 all-reduce.13.cloned.1.call-start
  22.8 571.7 %all-reduce.11.cloned.1.call-done = (f32[768,512]{1,0:T(8,128)}, f32[256,256]{1,0:T(8,128)}) async-done(((f32[768,512]{1,0:T(8,128)}, f32[256,256]{1,0:T(8,128)}), (f32[768,512]{1,0:T(8,128)}, f32[256,256]{1,0:T(8,128)})) %all-reduce.11.cloned.1.call-update) | async-done | bytes 1835024 | tf_op jit(solution)/shard_map/psum | solution.py:83
  594.5 0.0 all-reduce.13.cloned.1.call-update
  594.5 1.0 convolution_bitcast_fusion
  595.6 0.3 fusion.16
  595.9 0.0 copy-start.6
  595.9 0.2 pad_add_fusion
  596.2 1.3 collective-permute-start.1
  597.5 0.2 convert_reduce_fusion
  597.7 0.0 copy-done.6
  597.7 1.2 fusion.2
  598.8 4.8 collective-permute-done.1
  603.7 1.1 convert_reduce_fusion.1
  604.7 126.4 %all-reduce.4 = (f32[512]{0:T(512)S(1)}, f32[256]{0:T(256)S(1)}) all-reduce(f32[512]{0:T(512)S(1)} %convert_reduce_fusion, f32[256]{0:T(256)S(1)} %get-tuple-element.22), channel_id=1, replica_groups=mesh['tm'=64,'run'=8] {'tm'}, use_global_device_ids=true, to_apply=%region_3.4 | all-reduce | flops 768 | bytes 6144 | tf_op jit(solution)/shard_map/psum | solution.py:83
  731.1 84.9 %all-reduce.6 = (f32[512]{0:T(512)S(1)}, f32[256]{0:T(256)S(1)}) all-reduce(f32[512]{0:T(512)S(1)} %get-tuple-element.6, f32[256]{0:T(256)S(1)} %get-tuple-element.7), channel_id=1, replica_groups=mesh['tm'=64,'run'=8] {'run'}, use_global_device_ids=true, to_apply=%region_4.5 | all-reduce | flops 768 | bytes 6144 | tf_op jit(solution)/shard_map/psum | solution.py:83
  816.0 0.6 broadcast_multiply_fusion.3
  816.6 0.6 broadcast_multiply_fusion.2
  817.2 0.0 all-reduce.13.cloned.1.call-done
  817.2 0.0 copy-start.3
  817.2 2.8 broadcast_multiply_fusion
  820.0 0.0 copy-done.3
  820.0 0.7 broadcast_multiply_fusion.1
  (2 shorter events, 0.0 us)
Async XLA Ops:
  7.2 10.5 %copy-start = (bf16[768,512]{1,0:T(8,128)(2,1)S(1)}, bf16[768,512]{1,0:T(8,128)(2,1)}, u32[]{:S(2)}) copy-start(bf16[768,512]{1,0:T(8,128)(2,1)} %param.7) | copy-start | bytes 2359300
  7.2 10.5 %copy-start.2 = (bf16[1,1024,256]{2,1,0:T(8,128)(2,1)S(1)}, bf16[1,1024,256]{2,1,0:T(8,128)(2,1)}, u32[]{:S(2)}) copy-start(bf16[1,1024,256]{2,1,0:T(8,128)(2,1)} %param.6) | copy-start | bytes 1572868
  7.2 10.5 %copy-start.5 = (f32[512]{0:T(512)S(1)}, f32[512]{0:T(512)}, u32[]{:S(2)}) copy-start(f32[512]{0:T(512)} %param.8) | copy-start | bytes 6148
  7.2 587.3 %all-reduce.11.cloned.1.call-start = ((), (), s32[]{:S(2)}) async-start(), calls=%async_computation | async-start | bytes 3670016 | tf_op jit(solution)/shard_map/psum | solution.py:83
  8.3 8.1 collective-permute-start
  17.7 1.1 copy-start.1
  17.7 1.1 copy-start.4
  22.7 794.4 %all-reduce.13.cloned.1.call-start = ((), (), s32[]{:S(2)}) async-start(), calls=%async_computation.1 | async-start | bytes 3670016 | tf_op jit(solution)/shard_map/psum | solution.py:83
  595.9 1.8 copy-start.6
  596.2 7.5 collective-permute-start.1
  817.2 2.8 copy-start.3
Sparse Core Ops, SparseCore 0:
  22.9 571.6 all-reduce.10
  597.8 128.2 all-reduce.12
